TPU v7x, 32 devices: a whole 2x2x4 slice. The times are simulated.
32 devices in a mesh: prow: 8 (over y, x, core), pcol: 4 (over z).
Axes of the slice: x: 2, y: 2, z: 4, core: 2. Of those that a mesh axis runs over, the one named last changes fastest.
Arguments:
- matrix: float32 [4096, 4096], P('prow', 'pcol'), may hold values from -6 to 6
- pivots: int32 [2, 512], replicated, may hold values from 0 to 4095, as said below
- lower_inv: float32 [2, 512, 512], replicated, as said below
- upper_inv: float32 [2, 512, 512], replicated, as said below
Outputs:
- factored: float32 [4096, 4096], P('prow', 'pcol')
Inputs may be any that keep to these rules, and one draw needn't show every extreme that they name: The entries of pivots[k] are distinct row indices from k * 512 to 4095. Each lower_inv[k] is lower triangular. Each upper_inv[k] is upper triangular.
All inputs are finite; a program needn't handle non-finite values.
Results may differ from a plain program's by a relative error of at most 0.0001.
Values sent between devices are 32-bit elements; how exact they have to be, the bound alone decides.
No kernel may reach another device: no remote copies, remote signals or barrier semaphores. Data moves between devices by JAX's collectives and lax.ppermute only.
A program may use at most 128 MiB of HBM per device.

v0:
```python
import jax
import jax.numpy as jnp
from jax import lax
from jax.sharding import PartitionSpec as P


def broadcast(block, axis, holder):
    block = jnp.where(lax.axis_index(axis) == holder, block, jnp.zeros_like(block))
    return lax.psum(block, axis)


def displaced(pivot_row, start_row):
    width = pivot_row.shape[0]
    end_row = start_row + width
    window = start_row + jnp.arange(width, dtype=jnp.int32)
    chosen = jnp.any(pivot_row[None, :] == window[:, None], axis=1)
    unnamed = jnp.logical_not(chosen)
    free_rank = jnp.cumsum(unnamed.astype(jnp.int32)) - 1
    outside = pivot_row >= end_row
    out_rank = jnp.sum(
        (outside[None, :] & (pivot_row[None, :] < pivot_row[:, None])).astype(jnp.int32), axis=1
    )
    matches = unnamed[None, :] & (free_rank[None, :] == out_rank[:, None])
    source = jnp.sum(jnp.where(matches, window[None, :], 0), axis=1)
    return (source, outside)


def product(left, right):
    return jnp.dot(left, right, precision=lax.Precision.HIGHEST, preferred_element_type=jnp.float32)


def shards(matrix, pivots, lower_inv, upper_inv):
    local_rows, local_cols = matrix.shape
    block_width = lower_inv.shape[1]
    first_row = lax.axis_index("prow") * local_rows
    row_ids = first_row + jnp.arange(local_rows, dtype=jnp.int32)
    col_ids = lax.axis_index("pcol") * local_cols + jnp.arange(local_cols, dtype=jnp.int32)
    current = matrix
    for panel_index in range(pivots.shape[0]):
        start_row = panel_index * block_width
        end_row = start_row + block_width
        wanted = pivots[panel_index]
        offset = wanted - first_row
        owned_rows = (offset >= 0) & (offset < local_rows)
        gathered_rows = jnp.take(current, jnp.clip(offset, 0, local_rows - 1), axis=0)
        picked = jnp.where(owned_rows[:, None], gathered_rows, 0.0)
        beyond = col_ids >= end_row
        reduced = lax.psum_scatter(picked, "prow", scatter_dimension=0, tiled=True)
        raw_top = lax.all_gather(reduced, "prow", axis=0, tiled=True)
        solved = product(lower_inv[panel_index], raw_top)
        top_block = jnp.where(beyond[None, :], solved, raw_top)
        top_masked = jnp.where(beyond[None, :], solved, 0.0)
        owner_row = start_row // local_rows
        first_local = start_row - owner_row * local_rows
        local_top = current
        old_top = broadcast(local_top, "prow", owner_row)
        source, outside = displaced(wanted, start_row)
        dest_local = jnp.where(outside & owned_rows, offset, local_rows)
        moved = jnp.take(old_top, jnp.clip(source - start_row, 0, block_width - 1), axis=0)
        swapped = current.at[dest_local].set(moved, mode="drop")
        is_owner = lax.axis_index("prow") == owner_row
        top_slice = swapped
        swapped = swapped.at[first_local : first_local + block_width].set(
            jnp.where(is_owner, top_block, top_slice)
        )
        owner_col = start_row // local_cols
        left_col = start_row - owner_col * local_cols
        column_panel = product(
            swapped[:, left_col : left_col + block_width], upper_inv[panel_index]
        )
        lower_block = broadcast(column_panel, "pcol", owner_col)
        below_rows = row_ids >= end_row
        lower_masked = jnp.where(below_rows[:, None], lower_block, 0.0)
        updated = swapped - product(lower_masked, top_masked)
        panel_slice = updated[:, left_col : left_col + block_width]
        col_owner = lax.axis_index("pcol") == owner_col
        new_panel = jnp.where(below_rows[:, None] & col_owner, lower_block, panel_slice)
        current = updated.at[:, left_col : left_col + block_width].set(new_panel)
    return current


def solution(mesh):
    in_specs = (P("prow", "pcol"), P(), P(), P())
    out_specs = P("prow", "pcol")
    return jax.shard_map(shards, mesh=mesh, in_specs=in_specs, out_specs=out_specs, check_vma=False)
```

profile of v0, /device:TPU:0, one launch (start us, length us, event | category | flops | bytes accessed | tf_op | source)
XLA Modules:
  0.0 474.5 jit_solution(15905027569336554562)
XLA Ops:
  8.2 2.7 gather_fusion
  10.8 2.9 copy.50
  13.8 3.2 select_select_fusion.1
  17.0 2.9 copy.72
  21.8 3.1 broadcast_select_fusion.1
  25.0 39.0 %reduce-scatter.7.cloned.1.call-done = f32[64,1024]{1,0:T(8,128)} async-done(((f32[512,1024]{1,0:T(8,128)}), f32[64,1024]{1,0:T(8,128)}) %reduce-scatter.7.cloned.1.call-update) | async-done | bytes 262160 | tf_op jit(solution)/shard_map/reduce_scatter | solution.py:48
  65.9 63.2 %all-reduce.5.cloned.1.call-done = f32[512,1024]{0,1:T(8,128)} async-done(((f32[512,1024]{0,1:T(8,128)}), f32[512,1024]{0,1:T(8,128)}) %all-reduce.5.cloned.1.call-update) | async-done | bytes 2097168 | tf_op jit(solution)/shard_map/psum | solution.py:9
  129.0 2.9 copy.54
  131.9 19.5 %scatter_custom_fusion = f32[512,1024]{1,0:T(8,128)S(1)} fusion(f32[512,1024]{1,0:T(8,128)S(1)} %copy.85, s32[512]{0:T(512)S(1)} %bitcast.75, f32[]{:T(128)} %constant.160.clone.4, pred[512]{0:T(512)(128)(4,1)S(1)} %compare_and_fusion.2, f32[512,1024]{1,0:T(8,128)} %copy.54, s32[1024]{0:T(1024)S(1)} %pad_clamp_fusion.2), kind=kCustom, calls=%fused_computation.17 | custom fusion | flops 524288 | bytes 4198916 | tf_op jit(solution)/shard_map/scatter | solution.py:60
  153.2 5.0 %all-gather.3.cloned.1.call-done = f32[512,1024]{1,0:T(8,128)} async-done(((f32[64,1024]{1,0:T(8,128)}), f32[512,1024]{1,0:T(8,128)}) %all-gather.3.cloned.1.call-update) | async-done | bytes 2097168 | tf_op jit(solution)/shard_map/all_gather | solution.py:49
  158.2 2.9 copy.52
  161.1 10.8 %fusion.2 = (f32[512,1024]{0,1:T(8,128)S(1)}, f32[1024,512]{1,0:T(8,128)}) fusion(f32[512,1024]{0,1:T(8,128)} %copy.55, f32[512,1024]{0,1:T(8,128)} %copy.52, pred[1024]{0:T(1024)(128)(4,1)S(1)} %fusion.41, pred[]{:T(512)S(6)} %eq.31, f32[512,1024]{1,0:T(8,128)} %all-gather.3.cloned.1.call-done, f32[2,512,512]{2,1,0:T(8,128)} %param.20), kind=kOutput, calls=%fused_computation.12 | convolution fusion | flops 3222274048 | bytes 11535361 | tf_op jit(solution)/shard_map/dot_general | solution.py:29
  171.9 2.9 convolution_select_fusion.1
  175.7 51.7 %all-reduce.7.cloned.1.call-done = f32[512,512]{0,1:T(8,128)} async-done(((f32[512,512]{0,1:T(8,128)}), f32[512,512]{0,1:T(8,128)}) %all-reduce.7.cloned.1.call-update) | async-done | bytes 1048592 | tf_op jit(solution)/shard_map/psum | solution.py:9
  227.4 6.9 %fusion.8 = f32[512,1024]{0,1:T(8,128)} fusion(f32[512,1024]{0,1:T(8,128)S(1)} %get-tuple-element.86, f32[1024,512]{1,0:T(8,128)} %get-tuple-element.87, f32[512,512]{0,1:T(8,128)} %all-reduce.7.cloned.1.call-done, pred[1024]{0:T(1024)(128)(4,1)S(1)} %fusion.41, pred[512]{0:T(512)(128)(4,1)S(1)} %fusion.44), kind=kOutput, calls=%fused_computation.20 | convolution fusion | flops 3222536192 | bytes 7341568 | tf_op jit(solution)/shard_map/dot_general | solution.py:29
  234.3 3.0 fusion.10
  239.2 2.7 gather_fusion.1
  241.9 2.9 copy.59
  244.8 3.2 select_select_fusion
  248.0 2.9 copy.74
  252.6 39.1 %reduce-scatter.9.cloned.1.call-done = f32[64,1024]{1,0:T(8,128)} async-done(((f32[512,1024]{1,0:T(8,128)}), f32[64,1024]{1,0:T(8,128)}) %reduce-scatter.9.cloned.1.call-update) | async-done | bytes 262160 | tf_op jit(solution)/shard_map/reduce_scatter | solution.py:48
  293.0 63.5 %all-reduce.9.cloned.1.call-done = f32[512,1024]{0,1:T(8,128)} async-done(((f32[512,1024]{0,1:T(8,128)}), f32[512,1024]{0,1:T(8,128)}) %all-reduce.9.cloned.1.call-update) | async-done | bytes 2097168 | tf_op jit(solution)/shard_map/psum | solution.py:9
  356.5 2.9 copy.62
  359.4 19.6 %scatter_custom_fusion.1 = f32[512,1024]{1,0:T(8,128)S(1)} fusion(f32[512,1024]{1,0:T(8,128)S(1)} %copy.58, s32[512]{0:T(512)S(1)} %bitcast.74, f32[]{:T(128)} %constant.160.clone.4, pred[512]{0:T(512)(128)(4,1)S(1)} %compare_and_fusion, f32[512,1024]{1,0:T(8,128)} %copy.62, s32[1024]{0:T(1024)S(1)} %pad_clamp_fusion), kind=kCustom, calls=%fused_computation.14 | custom fusion | flops 524288 | bytes 4198916 | tf_op jit(solution)/shard_map/scatter | solution.py:60
  380.8 4.9 %all-gather.5.cloned.1.call-done = f32[512,1024]{1,0:T(8,128)} async-done(((f32[64,1024]{1,0:T(8,128)}), f32[512,1024]{1,0:T(8,128)}) %all-gather.5.cloned.1.call-update) | async-done | bytes 2097168 | tf_op jit(solution)/shard_map/all_gather | solution.py:49
  385.7 3.1 copy.61
  388.8 11.4 %fusion = (f32[512,1024]{0,1:T(8,128)S(1)}, f32[1024,512]{1,0:T(8,128)}) fusion(f32[512,1024]{0,1:T(8,128)} %copy.64, f32[512,1024]{0,1:T(8,128)} %copy.61, pred[1024]{0:T(1024)(128)(4,1)S(1)} %fusion.42, pred[]{:T(512)S(6)} %eq.30, f32[512,1024]{1,0:T(8,128)} %all-gather.5.cloned.1.call-done, f32[2,512,512]{2,1,0:T(8,128)} %param.20), kind=kOutput, calls=%fused_computation.8 | convolution fusion | flops 3222274048 | bytes 11535361 | tf_op jit(solution)/shard_map/dot_general | solution.py:29
  400.3 2.9 convolution_select_fusion
  403.2 51.9 %all-reduce.11.cloned.1.call-done = f32[512,512]{0,1:T(8,128)} async-done(((f32[512,512]{0,1:T(8,128)}), f32[512,512]{0,1:T(8,128)}) %all-reduce.11.cloned.1.call-update) | async-done | bytes 1048592 | tf_op jit(solution)/shard_map/psum | solution.py:9
  455.2 6.9 %fusion.9 = f32[512,1024]{0,1:T(8,128)} fusion(f32[512,1024]{0,1:T(8,128)S(1)} %get-tuple-element.88, f32[1024,512]{1,0:T(8,128)} %get-tuple-element.89, f32[512,512]{0,1:T(8,128)} %all-reduce.11.cloned.1.call-done, pred[1024]{0:T(1024)(128)(4,1)S(1)} %fusion.42, pred[512]{0:T(512)(128)(4,1)S(1)} %fusion.43), kind=kOutput, calls=%fused_computation.21 | convolution fusion | flops 3222536192 | bytes 7341568 | tf_op jit(solution)/shard_map/dot_general | solution.py:29
  462.1 2.5 fusion.11
  464.5 2.9 copy.67
  (70 shorter events, 14.9 us)
Async XLA Ops:
  6.5 1.6 copy-start.4
  6.5 57.4 %reduce-scatter.7.cloned.1.call-start = ((), (), s32[]{:S(2)}) async-start(), calls=%async_computation.8 | async-start | bytes 2359296 | tf_op jit(solution)/shard_map/reduce_scatter | solution.py:48
  19.9 109.1 %all-reduce.5.cloned.1.call-start = ((), (), s32[]{:S(2)}) async-start(), calls=%async_computation.3 | async-start | bytes 4194304 | tf_op jit(solution)/shard_map/psum | solution.py:9
  25.0 133.2 %all-gather.3.cloned.1.call-start = ((), (), s32[]{:S(2)}) async-start(), calls=%async_computation.2 | async-start | bytes 2359296 | tf_op jit(solution)/shard_map/all_gather | solution.py:49
  64.0 163.4 %all-reduce.7.cloned.1.call-start = ((), (), s32[]{:S(2)}) async-start(), calls=%async_computation.4 | async-start | bytes 2097152 | tf_op jit(solution)/shard_map/psum | solution.py:9
  161.1 10.8 %copy-start.2 = (f32[2,512,512]{2,1,0:T(8,128)S(1)}, f32[2,512,512]{2,1,0:T(8,128)}, u32[]{:S(2)}) copy-start(f32[2,512,512]{2,1,0:T(8,128)} %param.21) | copy-start | bytes 6291460
  174.8 116.8 %reduce-scatter.9.cloned.1.call-start = ((), (), s32[]{:S(2)}) async-start(), calls=%async_computation.9 | async-start | bytes 2359296 | tf_op jit(solution)/shard_map/reduce_scatter | solution.py:48
  227.4 6.9 %copy-start = (f32[512,512]{0,1:T(8,128)S(1)}, f32[512,512]{0,1:T(8,128)}, u32[]{:S(2)}) copy-start(f32[512,512]{0,1:T(8,128)} %all-reduce.7.cloned.1.call-done) | copy-start | bytes 3145732
  250.9 105.7 %all-reduce.9.cloned.1.call-start = ((), (), s32[]{:S(2)}) async-start(), calls=%async_computation.6 | async-start | bytes 4194304 | tf_op jit(solution)/shard_map/psum | solution.py:9
  252.5 133.2 %all-gather.5.cloned.1.call-start = ((), (), s32[]{:S(2)}) async-start(), calls=%async_computation.5 | async-start | bytes 2359296 | tf_op jit(solution)/shard_map/all_gather | solution.py:49
  291.7 163.5 %all-reduce.11.cloned.1.call-start = ((), (), s32[]{:S(2)}) async-start(), calls=%async_computation.7 | async-start | bytes 2097152 | tf_op jit(solution)/shard_map/psum | solution.py:9
  388.8 11.4 %copy-start.3 = (f32[2,512,512]{2,1,0:T(8,128)S(1)}, f32[2,512,512]{2,1,0:T(8,128)}, u32[]{:S(2)}) copy-start(f32[2,512,512]{2,1,0:T(8,128)} %param.21) | copy-start | bytes 6291460
  455.2 6.9 %copy-start.1 = (f32[512,512]{0,1:T(8,128)S(1)}, f32[512,512]{0,1:T(8,128)}, u32[]{:S(2)}) copy-start(f32[512,512]{0,1:T(8,128)} %all-reduce.11.cloned.1.call-done) | copy-start | bytes 3145732
Sparse Core Ops, SparseCore 0:
  20.0 43.8 reduce-scatter.6
  67.5 61.4 all-reduce.4
  131.1 27.0 all-gather.2
  175.0 52.4 all-reduce.6
  251.0 40.5 reduce-scatter.8
  295.1 61.4 all-reduce.8
  358.6 27.0 all-gather.4
  403.3 51.8 all-reduce.10
where the time goes:
time: 482 us; the launch traced here: 474 us
  waiting for transfers between devices  318 us (66%)
  other arithmetic  59 us (12%)
  matrix products  41.9 us (9%)
  local copies, waits for them, and re-layouts  41 us (9%)
  between operations  13.9 us (3%)
    psum x4, waiting for transfers between devices, broadcast(): return lax.psum(block, axis)  230 us
    reduce_scatter x2, waiting for transfers between devices, shards(): reduced = lax.psum_scatter(picked, 'prow', scatter_dimension=0, tiled=True)  78 us
    dot_general x6, matrix products, product(): jnp.dot(left, right, precision=lax.Precision.HIGHEST, preferred_element_t...  41.9 us
    scatter x2, other arithmetic, shards(): swapped = current.at[dest_local].set(moved, mode='drop')  39.1 us
    gather x4, local copies, waits for them, and re-layouts, shards(): jnp.take(current, jnp.clip(offset, 0, local_rows - 1), axis=0)  11.1 us
    all_gather x2, waiting for transfers between devices, shards(): raw_top = lax.all_gather(reduced, 'prow', axis=0, tiled=True)  9.83 us
  transfers between devices with their start and end apart: 8, of which 8 were waited for; matrix products, arithmetic and copies ran while one was open for 12% of the time, Pallas kernels for 0%

commit v1 on v0

--- a/solution.py
+++ b/solution.py
@@ -6,7 +6,12 @@
 
 def broadcast(block, axis, holder):
     block = jnp.where(lax.axis_index(axis) == holder, block, jnp.zeros_like(block))
-    return lax.psum(block, axis)
+
+    def mark_block(local_array, ax_name):
+        n_now = lax.all_gather(local_array, axis_name=ax_name)
+        return jnp.sum(n_now, axis=0)
+
+    return mark_block(block, axis)
 
 
 def displaced(pivot_row, start_row):

time: 482 us -> 713 us (1.48)
  waiting for transfers between devices: 318 us -> 473 us
  local copies, waits for them, and re-layouts: 41 us -> 91.4 us
  other arithmetic: 59 us -> 84.2 us
    all_gather x0 -> x4, waiting for transfers between devices: none -> 339 us  [mark_block(): n_now = lax.all_gather(local_array, axis_name=ax_name)]
    psum x4 -> x0, waiting for transfers between devices: 230 us -> none  [broadcast(): return lax.psum(block, axis)]
    all_gather x2, waiting for transfers between devices: 9.83 us -> 49.6 us  [shards(): raw_top = lax.all_gather(reduced, 'prow', axis=0, tiled=True)]
    unnamed x14 -> x12, local copies, waits for them, and re-layouts: 9.27 us -> 47.5 us
    reduce_sum x0 -> x4, other arithmetic: none -> 25.4 us  [mark_block(): return jnp.sum(n_now, axis=0)]
    all_gather x0 -> x2, local copies, waits for them, and re-layouts: none -> 12.3 us  [mark_block(): n_now = lax.all_gather(local_array, axis_name=ax_name)]
  transfers between devices with their start and end apart: 8 -> 8, of which waited for: 8 -> 8; matrix products, arithmetic and copies ran while one was open for 12% -> 2% of each run, Pallas kernels for 0% -> 0%
where the time goes in v1:
time: 713 us; the launch traced here: 705 us
  waiting for transfers between devices  473 us (66%)
  local copies, waits for them, and re-layouts  91.4 us (13%)
  other arithmetic  84.2 us (12%)
  matrix products  41 us (6%)
  between operations  14.1 us (2%)
    all_gather x4, waiting for transfers between devices, mark_block(): n_now = lax.all_gather(local_array, axis_name=ax_name)  339 us
    reduce_scatter x2, waiting for transfers between devices, shards(): reduced = lax.psum_scatter(picked, 'prow', scatter_dimension=0, tiled=True)  83.9 us
    all_gather x2, waiting for transfers between devices, shards(): raw_top = lax.all_gather(reduced, 'prow', axis=0, tiled=True)  49.6 us
    unnamed x12, local copies, waits for them, and re-layouts  47.5 us
    dot_general x6, matrix products, product(): jnp.dot(left, right, precision=lax.Precision.HIGHEST, preferred_element_t...  41 us
    scatter x2, other arithmetic, shards(): swapped = current.at[dest_local].set(moved, mode='drop')  39 us
    reduce_sum x4, other arithmetic, mark_block(): return jnp.sum(n_now, axis=0)  25.4 us
  transfers between devices with their start and end apart: 8, of which 8 were waited for; matrix products, arithmetic and copies ran while one was open for 2% of the time, Pallas kernels for 0%

profile of v1, /device:TPU:0, one launch (start us, length us, event | category | flops | bytes accessed | tf_op | source)
XLA Modules:
  0.0 704.5 jit_solution(2652224312785736082)
XLA Ops:
  10.8 2.9 copy.46
  13.8 3.2 select_select_fusion.1
  17.0 2.9 copy.68
  20.0 44.0 %reduce-scatter.7.cloned.1.call-done = f32[64,1024]{1,0:T(8,128)} async-done(((f32[512,1024]{1,0:T(8,128)}), f32[64,1024]{1,0:T(8,128)}) %reduce-scatter.7.cloned.1.call-update) | async-done | bytes 262160 | tf_op jit(solution)/shard_map/reduce_scatter | solution.py:53
  65.9 3.1 broadcast_select_fusion.1
  70.9 23.1 %all-gather.11.cloned.1.call-done = f32[512,1024]{1,0:T(8,128)} async-done(((f32[64,1024]{1,0:T(8,128)}), f32[512,1024]{1,0:T(8,128)}) %all-gather.11.cloned.1.call-update) | async-done | bytes 2097168 | tf_op jit(solution)/shard_map/all_gather | solution.py:54
  96.9 89.1 %all-gather.15.cloned.1.call-done = f32[4096,1024]{0,1:T(8,128)} async-done(((f32[512,1024]{0,1:T(8,128)}), f32[4096,1024]{0,1:T(8,128)}) %all-gather.15.cloned.1.call-update) | async-done | bytes 16777232 | tf_op jit(solution)/shard_map/all_gather | solution.py:11
  185.9 19.1 %copy.72 = f32[128,8,8,512]{3,2,1,0:T(8,128)S(1)} copy(f32[128,8,8,512]{3,1,2,0:T(8,128)} %bitcast.82) | data formatting | bytes 33554432
  205.1 8.0 %bitcast_reduce_fusion.1 = f32[512,1024]{0,1:T(8,128)} fusion(f32[128,8,8,512]{3,2,1,0:T(8,128)S(1)} %copy.72), kind=kLoop, calls=%fused_computation.7 | loop fusion | flops 3670016 | bytes 18874368 | tf_op jit(solution)/shard_map/reduce_sum | solution.py:12
  213.1 2.9 copy.50
  216.0 19.2 %scatter_custom_fusion = f32[512,1024]{1,0:T(8,128)S(1)} fusion(f32[512,1024]{1,0:T(8,128)S(1)} %copy.79, s32[512]{0:T(512)S(1)} %bitcast.91, f32[]{:T(128)} %constant.160.clone.4, pred[512]{0:T(512)(128)(4,1)S(1)} %compare_and_fusion.2, f32[512,1024]{1,0:T(8,128)} %copy.50, s32[1024]{0:T(1024)S(1)} %pad_clamp_fusion.2), kind=kCustom, calls=%fused_computation.19 | custom fusion | flops 524288 | bytes 4198916 | tf_op jit(solution)/shard_map/scatter | solution.py:65
  237.0 10.8 %fusion.2 = (f32[512,1024]{0,1:T(8,128)S(1)}, f32[1024,512]{1,0:T(8,128)}) fusion(f32[512,1024]{0,1:T(8,128)} %copy.51, f32[512,1024]{0,1:T(8,128)} %copy.48, pred[1024]{0:T(1024)(128)(4,1)S(1)} %fusion.41, pred[]{:T(512)S(6)} %eq.31, f32[512,1024]{1,0:T(8,128)} %all-gather.11.cloned.1.call-done, f32[2,512,512]{2,1,0:T(8,128)} %param.20), kind=kOutput, calls=%fused_computation.14 | convolution fusion | flops 3222274048 | bytes 11535361 | tf_op jit(solution)/shard_map/dot_general | solution.py:34
  247.8 2.9 convolution_select_fusion.1
  252.0 80.4 %all-gather.17.cloned.1.call-done = f32[2048,512]{0,1:T(8,128)} async-done(((f32[512,512]{0,1:T(8,128)}), f32[2048,512]{0,1:T(8,128)}) %all-gather.17.cloned.1.call-update) | async-done | bytes 4194320 | tf_op jit(solution)/shard_map/all_gather | solution.py:11
  332.3 6.0 reshape.355
  338.3 4.7 reduce_sum.75
  343.0 6.5 fusion.8
  349.5 3.0 fusion.10
  360.0 3.2 select_select_fusion
  366.1 39.9 %reduce-scatter.9.cloned.1.call-done = f32[64,1024]{1,0:T(8,128)} async-done(((f32[512,1024]{1,0:T(8,128)}), f32[64,1024]{1,0:T(8,128)}) %reduce-scatter.9.cloned.1.call-update) | async-done | bytes 262160 | tf_op jit(solution)/shard_map/reduce_scatter | solution.py:53
  409.2 26.5 %all-gather.13.cloned.1.call-done = f32[512,1024]{1,0:T(8,128)} async-done(((f32[64,1024]{1,0:T(8,128)}), f32[512,1024]{1,0:T(8,128)}) %all-gather.13.cloned.1.call-update) | async-done | bytes 2097168 | tf_op jit(solution)/shard_map/all_gather | solution.py:54
  438.6 88.9 %all-gather.19.cloned.1.call-done = f32[4096,1024]{0,1:T(8,128)} async-done(((f32[512,1024]{0,1:T(8,128)}), f32[4096,1024]{0,1:T(8,128)}) %all-gather.19.cloned.1.call-update) | async-done | bytes 16777232 | tf_op jit(solution)/shard_map/all_gather | solution.py:11
  527.5 19.1 %copy.73 = f32[128,8,8,512]{3,2,1,0:T(8,128)S(1)} copy(f32[128,8,8,512]{3,1,2,0:T(8,128)} %bitcast.83) | data formatting | bytes 33554432
  546.6 8.0 %bitcast_reduce_fusion = f32[512,1024]{0,1:T(8,128)} fusion(f32[128,8,8,512]{3,2,1,0:T(8,128)S(1)} %copy.73), kind=kLoop, calls=%fused_computation.6 | loop fusion | flops 3670016 | bytes 18874368 | tf_op jit(solution)/shard_map/reduce_sum | solution.py:12
  554.6 2.9 copy.58
  557.6 19.8 %scatter_custom_fusion.1 = f32[512,1024]{1,0:T(8,128)S(1)} fusion(f32[512,1024]{1,0:T(8,128)S(1)} %copy.54, s32[512]{0:T(512)S(1)} %bitcast.90, f32[]{:T(128)} %constant.160.clone.4, pred[512]{0:T(512)(128)(4,1)S(1)} %compare_and_fusion, f32[512,1024]{1,0:T(8,128)} %copy.58, s32[1024]{0:T(1024)S(1)} %pad_clamp_fusion), kind=kCustom, calls=%fused_computation.16 | custom fusion | flops 524288 | bytes 4198916 | tf_op jit(solution)/shard_map/scatter | solution.py:65
  579.2 11.4 %fusion = (f32[512,1024]{0,1:T(8,128)S(1)}, f32[1024,512]{1,0:T(8,128)}) fusion(f32[512,1024]{0,1:T(8,128)} %copy.60, f32[512,1024]{0,1:T(8,128)} %copy.57, pred[1024]{0:T(1024)(128)(4,1)S(1)} %fusion.42, pred[]{:T(512)S(6)} %eq.30, f32[512,1024]{1,0:T(8,128)} %all-gather.13.cloned.1.call-done, f32[2,512,512]{2,1,0:T(8,128)} %param.20), kind=kOutput, calls=%fused_computation.10 | convolution fusion | flops 3222274048 | bytes 11535361 | tf_op jit(solution)/shard_map/dot_general | solution.py:34
  590.6 2.9 convolution_select_fusion
  593.6 80.9 %all-gather.21.cloned.1.call-done = f32[2048,512]{0,1:T(8,128)} async-done(((f32[512,512]{0,1:T(8,128)}), f32[2048,512]{0,1:T(8,128)}) %all-gather.21.cloned.1.call-update) | async-done | bytes 4194320 | tf_op jit(solution)/shard_map/all_gather | solution.py:11
  674.5 6.2 reshape.357
  680.7 4.7 reduce_sum.79
  685.4 6.5 fusion.9
  (74 shorter events, 37.5 us)
Async XLA Ops:
  6.5 1.6 copy-start.2
  6.5 57.4 %reduce-scatter.7.cloned.1.call-start = ((), (), s32[]{:S(2)}) async-start(), calls=%async_computation.8 | async-start | bytes 2359296 | tf_op jit(solution)/shard_map/reduce_scatter | solution.py:53
  19.9 74.0 %all-gather.11.cloned.1.call-start = ((), (), s32[]{:S(2)}) async-start(), calls=%async_computation.2 | async-start | bytes 2359296 | tf_op jit(solution)/shard_map/all_gather | solution.py:54
  64.0 121.9 %all-gather.15.cloned.1.call-start = ((), (), s32[]{:S(2)}) async-start(), calls=%async_computation.4 | async-start | bytes 18874368 | tf_op jit(solution)/shard_map/all_gather | solution.py:11
  69.0 263.3 %all-gather.17.cloned.1.call-start = ((), (), s32[]{:S(2)}) async-start(), calls=%async_computation.5 | async-start | bytes 5242880 | tf_op jit(solution)/shard_map/all_gather | solution.py:11
  237.0 10.8 %copy-start = (f32[2,512,512]{2,1,0:T(8,128)S(1)}, f32[2,512,512]{2,1,0:T(8,128)}, u32[]{:S(2)}) copy-start(f32[2,512,512]{2,1,0:T(8,128)} %param.21) | copy-start | bytes 6291460
  250.8 155.2 %reduce-scatter.9.cloned.1.call-start = ((), (), s32[]{:S(2)}) async-start(), calls=%async_computation.9 | async-start | bytes 2359296 | tf_op jit(solution)/shard_map/reduce_scatter | solution.py:53
  366.1 69.6 %all-gather.13.cloned.1.call-start = ((), (), s32[]{:S(2)}) async-start(), calls=%async_computation.3 | async-start | bytes 2359296 | tf_op jit(solution)/shard_map/all_gather | solution.py:54
  406.0 121.5 %all-gather.19.cloned.1.call-start = ((), (), s32[]{:S(2)}) async-start(), calls=%async_computation.6 | async-start | bytes 18874368 | tf_op jit(solution)/shard_map/all_gather | solution.py:11
  407.7 266.8 %all-gather.21.cloned.1.call-start = ((), (), s32[]{:S(2)}) async-start(), calls=%async_computation.7 | async-start | bytes 5242880 | tf_op jit(solution)/shard_map/all_gather | solution.py:11
  579.2 11.4 %copy-start.1 = (f32[2,512,512]{2,1,0:T(8,128)S(1)}, f32[2,512,512]{2,1,0:T(8,128)}, u32[]{:S(2)}) copy-start(f32[2,512,512]{2,1,0:T(8,128)} %param.21) | copy-start | bytes 6291460
Sparse Core Ops, SparseCore 0:
  20.0 43.8 reduce-scatter.6
  66.0 27.8 all-gather.10
  96.0 89.8 all-gather.14
  250.9 81.3 all-gather.16
  366.2 39.7 reduce-scatter.8
  407.8 27.8 all-gather.12
  437.6 89.8 all-gather.18
  593.7 80.7 all-gather.20
